TPU v7x, 32 devices: a whole 2x2x4 slice. The times are simulated.
32 devices in a mesh: dp: 8 (over z, y), rep: 4 (over x, core).
Axes of the slice: x: 2, y: 2, z: 4, core: 2. Of those that a mesh axis runs over, the one named last changes fastest.
Arguments:
- image_tokens: bfloat16 [256, 50, 768], P(('dp', 'rep')), may hold values from -6 to 6
- image_weights: bfloat16 [768, 9216], P('dp'), may hold values from -1 to 1
- image_vectors: float32 [9216], replicated, may hold values from -0.8 to 1.4
- text_tokens: bfloat16 [64, 64, 768], P(('dp', 'rep')), may hold values from -6 to 6
- segments: int32 [64, 64], P(('dp', 'rep')), may hold values from 0 to 3, never falling along the last dimension, each value on 1 to 28 neighbouring positions
- text_weights: float32 [768, 9216], P('dp'), may hold values from -1 to 1
- text_vectors: float32 [9216], replicated, may hold values from -0.8 to 1.4
- momentum: float32 [768, 9216], P('dp'), may hold values from -0.5 to 0.5
- vector_momentum: float32 [9216], replicated, may hold values from -2.5 to 2.5
- error_feedback: float32 [4, 768, 9216], P('rep', 'dp'), may hold values from -2.5 to 2.5
- start_factors: float32 [8, 9216], replicated, may hold values from -6 to 6
Outputs:
- contrast_loss: float32 [], replicated
- text_output: float32 [64, 64, 768], P(('dp', 'rep'))
- text_input_grad: float32 [64, 64, 768], P(('dp', 'rep'))
- new_weights: float32 [768, 9216], P('dp')
- new_momentum: float32 [768, 9216], P('dp')
- new_feedback: float32 [4, 768, 9216], P('rep', 'dp')
- new_vectors: float32 [9216], replicated
- new_vector_momentum: float32 [9216], replicated
- left_factors: float32 [32, 768], replicated
- right_factors: float32 [8, 9216], replicated
Inputs may be any that keep to these rules, and one draw needn't show every extreme that they name: `segments`: each row holds 4 captions numbered in order, each of 1 to 28 tokens, some caption of exactly 28.
All inputs are finite; a program needn't handle non-finite values.
Results may differ from a plain program's by a relative error of at most 0.015.
The roundings to bfloat16 on the way count: a program that leaves them out, or rounds other values in their place, can miss the bound.
Values may be sent and summed in bfloat16 or wider, within the bound.
A program may use at most 192 MiB of HBM per device.

v0:
```python
import jax
import jax.numpy as jnp
from jax import lax
from jax.sharding import PartitionSpec as P

D = 768
FF = 3072
HEADS = 12
HEAD_DIM = 64
PER_ROW = 4


PRECISE = lax.Precision.HIGHEST
LAYER_EPS = 1e-06
SCORE_SCALE = 0.125
LOGIT_SCALE = 50.0
MOMENTUM_DECAY = 0.9
STEP_RATE = 0.08
NORM_FLOOR = 1e-08
MASKED = -1e30


def layer_norm(values, layer_gain, layer_shift):
    center = values - jnp.mean(values, axis=-1, keepdims=True)
    spread = jnp.mean(center * center, axis=-1, keepdims=True)
    return center * lax.rsqrt(spread + LAYER_EPS) * layer_gain + layer_shift


def unit_rows(values):
    return values * lax.rsqrt(jnp.sum(values * values, axis=-1, keepdims=True) + LAYER_EPS)


def vector_parts(vectors):
    pieces = [vectors[position * D : (position + 1) * D] for position in range(8)]
    return pieces + [vectors[8 * D :]]


def matrix_bounds():
    return ((0, 3 * D), (3 * D, 4 * D), (4 * D, 4 * D + FF), (4 * D + FF, 4 * D + 2 * FF))


def row_log_total(values):
    highest = jnp.max(values, axis=1, keepdims=True)
    return highest[:, 0] + jnp.log(jnp.sum(jnp.exp(values - highest), axis=1))


def masked_scores(query_heads, key_heads, allowed):
    scores = (
        jnp.einsum("rshd,rthd->rhst", query_heads, key_heads, preferred_element_type=jnp.float32)
        * SCORE_SCALE
    )
    return jnp.where(allowed[:, None], scores, MASKED)


def block_forward(inputs, allowed, weights, vector_pieces):
    (
        gain_one,
        shift_one,
        bias_query,
        bias_value,
        bias_out,
        gain_two,
        shift_two,
        bias_shrink,
        bias_expand,
    ) = vector_pieces
    row_count, seq_tokens = (inputs.shape[0], inputs.shape[1])
    normed = layer_norm(inputs, gain_one, shift_one).astype(jnp.bfloat16)
    mixing = jnp.einsum(
        "rsd,dc->rsc", normed, weights[:, : 3 * D], preferred_element_type=jnp.float32
    )
    mixing = mixing + jnp.concatenate([bias_query, jnp.zeros_like(bias_query), bias_value])
    head_parts = mixing.astype(jnp.bfloat16).reshape(row_count, seq_tokens, 3, HEADS, HEAD_DIM)
    query_heads, key_heads, value_heads = (
        head_parts[:, :, 0],
        head_parts[:, :, 1],
        head_parts[:, :, 2],
    )
    scores = masked_scores(query_heads, key_heads, allowed)
    highest = jnp.max(scores, axis=-1, keepdims=True)
    log_total = highest + jnp.log(jnp.sum(jnp.exp(scores - highest), axis=-1, keepdims=True))
    attention = jnp.exp(scores - log_total).astype(jnp.bfloat16)
    mixed_heads = jnp.einsum(
        "rhst,rthd->rshd", attention, value_heads, preferred_element_type=jnp.float32
    )
    mixed_heads = mixed_heads.reshape(row_count, seq_tokens, D).astype(jnp.bfloat16)
    attended = (
        jnp.einsum(
            "rsd,de->rse",
            mixed_heads,
            weights[:, 3 * D : 4 * D],
            preferred_element_type=jnp.float32,
        )
        + bias_out
    )
    middle = inputs + attended
    normed_two = layer_norm(middle, gain_two, shift_two).astype(jnp.bfloat16)
    hidden = (
        jnp.einsum(
            "rsd,df->rsf",
            normed_two,
            weights[:, 4 * D : 4 * D + FF],
            preferred_element_type=jnp.float32,
        )
        + bias_expand
    )
    active = jax.nn.gelu(hidden, approximate=False).astype(jnp.bfloat16)
    shrunk = (
        jnp.einsum(
            "rsf,df->rsd", active, weights[:, 4 * D + FF :], preferred_element_type=jnp.float32
        )
        + bias_shrink
    )
    forward_kept = (
        normed,
        query_heads,
        key_heads,
        value_heads,
        log_total,
        mixed_heads,
        middle,
        normed_two,
        hidden,
        active,
    )
    return (middle + shrunk, forward_kept)


def token_sum(values_low):
    return jnp.sum(values_low.astype(jnp.float32).reshape(-1, values_low.shape[-1]), axis=0)


def block_backward(inputs, allowed, weights, vector_pieces, forward_kept, grad_out):
    (
        gain_one,
        shift_one,
        bias_query,
        bias_value,
        bias_out,
        gain_two,
        shift_two,
        bias_shrink,
        bias_expand,
    ) = vector_pieces
    (
        normed,
        query_heads,
        key_heads,
        value_heads,
        log_total,
        mixed_heads,
        middle,
        normed_two,
        hidden,
        active,
    ) = forward_kept
    row_count, seq_tokens = (inputs.shape[0], inputs.shape[1])
    grad_shrunk = grad_out.astype(jnp.bfloat16)
    grad_active = jnp.einsum(
        "rsd,df->rsf", grad_shrunk, weights[:, 4 * D + FF :], preferred_element_type=jnp.float32
    )
    _, gelu_back = jax.vjp(lambda before_gelu: jax.nn.gelu(before_gelu, approximate=False), hidden)
    grad_hidden = gelu_back(grad_active)[0].astype(jnp.bfloat16)
    grad_normed_two = jnp.einsum(
        "rsf,df->rsd",
        grad_hidden,
        weights[:, 4 * D : 4 * D + FF],
        preferred_element_type=jnp.float32,
    )
    _, norm_two_back = jax.vjp(layer_norm, middle, gain_two, shift_two)
    grad_middle, grad_gain_two, grad_shift_two = norm_two_back(grad_normed_two)
    grad_middle = grad_middle + grad_out
    grad_attended = grad_middle.astype(jnp.bfloat16)
    grad_mixed = jnp.einsum(
        "rse,de->rsd", grad_attended, weights[:, 3 * D : 4 * D], preferred_element_type=jnp.float32
    )
    grad_mixed = grad_mixed.astype(jnp.bfloat16).reshape(row_count, seq_tokens, HEADS, HEAD_DIM)
    attention = jnp.exp(masked_scores(query_heads, key_heads, allowed) - log_total)
    grad_values = jnp.einsum(
        "rhst,rshd->rthd",
        attention.astype(jnp.bfloat16),
        grad_mixed,
        preferred_element_type=jnp.float32,
    )
    grad_attention = jnp.einsum(
        "rshd,rthd->rhst", grad_mixed, value_heads, preferred_element_type=jnp.float32
    )
    grad_scores = attention * (
        grad_attention - jnp.sum(attention * grad_attention, axis=-1, keepdims=True)
    )
    grad_scores = grad_scores.astype(jnp.bfloat16)
    grad_query = (
        jnp.einsum("rhst,rthd->rshd", grad_scores, key_heads, preferred_element_type=jnp.float32)
        * SCORE_SCALE
    )
    grad_keys = (
        jnp.einsum("rhst,rshd->rthd", grad_scores, query_heads, preferred_element_type=jnp.float32)
        * SCORE_SCALE
    )
    grad_mixing = (
        jnp.stack([grad_query, grad_keys, grad_values], axis=2)
        .reshape(row_count, seq_tokens, 3 * D)
        .astype(jnp.bfloat16)
    )
    grad_normed = jnp.einsum(
        "rsc,dc->rsd", grad_mixing, weights[:, : 3 * D], preferred_element_type=jnp.float32
    )
    _, norm_one_back = jax.vjp(layer_norm, inputs, gain_one, shift_one)
    grad_inputs, grad_gain_one, grad_shift_one = norm_one_back(grad_normed)
    grad_inputs = grad_inputs + grad_middle
    vector_grad = jnp.concatenate(
        [
            grad_gain_one,
            grad_shift_one,
            token_sum(grad_mixing[..., :D]),
            token_sum(grad_mixing[..., 2 * D :]),
            token_sum(grad_attended),
            grad_gain_two,
            grad_shift_two,
            token_sum(grad_shrunk),
            token_sum(grad_hidden),
        ]
    )
    tokens = row_count * seq_tokens
    outer_terms = (
        (normed.reshape(tokens, D), grad_mixing.reshape(tokens, 3 * D)),
        (mixed_heads.reshape(tokens, D), grad_attended.reshape(tokens, D)),
        (normed_two.reshape(tokens, D), grad_hidden.reshape(tokens, FF)),
        (grad_shrunk.reshape(tokens, D), active.reshape(tokens, FF)),
    )
    return (grad_inputs, vector_grad, outer_terms)


def orthonormal(stacked):
    finished = []
    for column_id in range(stacked.shape[1]):
        vector = stacked[:, column_id]
        for earlier in finished:
            vector = vector - jnp.sum(earlier * vector, axis=-1, keepdims=True) * earlier
        vector = vector / (jnp.sqrt(jnp.sum(vector * vector, axis=-1, keepdims=True)) + NORM_FLOOR)
        finished.append(vector)
    return jnp.stack(finished, axis=1)


def rows_factor(start_part, row_block):
    return jnp.einsum("kc,dc->kd", start_part, row_block, precision=PRECISE)


def per_device(
    image_tokens,
    image_weights,
    image_vectors,
    text_tokens,
    segments,
    text_weights,
    text_vectors,
    momentum,
    vector_momentum,
    error_feedback,
    start_factors,
):
    rep_count = lax.axis_size("rep")
    device_pairs = image_tokens.shape[0]
    patches = image_tokens.shape[1]
    pair_total = device_pairs * lax.axis_size("dp") * rep_count
    own_rows = text_weights.shape[0]
    row_start = lax.axis_index("dp") * own_rows
    factor_rank = start_factors.shape[0]
    bounds = matrix_bounds()
    text_low, frozen = (
        lax.all_gather(text_weights.astype(jnp.bfloat16), "dp", axis=0, tiled=True),
        lax.all_gather(image_weights, "dp", axis=0, tiled=True),
    )
    full_mask = jnp.zeros((device_pairs, patches, patches), jnp.int32) == 0
    image_out, _ = block_forward(
        image_tokens.astype(jnp.float32), full_mask, frozen, vector_parts(image_vectors)
    )
    image_emb = unit_rows(jnp.mean(image_out, axis=1)).astype(jnp.bfloat16)
    text_float = text_tokens.astype(jnp.float32)
    allowed = segments[:, :, None] == segments[:, None, :]
    vector_pieces = vector_parts(text_vectors)
    text_output, forward_kept = block_forward(text_float, allowed, text_low, vector_pieces)
    caption_marks = (
        segments[:, None, :] == jnp.arange(PER_ROW, dtype=jnp.int32)[None, :, None]
    ).astype(jnp.float32)
    counts = jnp.sum(caption_marks, axis=-1, keepdims=True)
    pooled = (
        jnp.einsum("rks,rsd->rkd", caption_marks, text_output, precision=PRECISE) / counts
    ).reshape(-1, D)
    text_norm, embed_back = jax.vjp(unit_rows, pooled)
    text_emb = text_norm.astype(jnp.bfloat16)
    image_all, text_all = (
        lax.all_gather(image_emb, ("dp", "rep"), axis=0, tiled=True),
        lax.all_gather(text_emb, ("dp", "rep"), axis=0, tiled=True),
    )
    offset = lax.axis_index(("dp", "rep")) * device_pairs
    diagonal_pick = (
        jnp.arange(pair_total, dtype=jnp.int32)[None, :]
        == offset + jnp.arange(device_pairs, dtype=jnp.int32)[:, None]
    ).astype(jnp.float32)
    image_logits = LOGIT_SCALE * jnp.einsum(
        "pd,bd->pb", image_emb, text_all, preferred_element_type=jnp.float32
    )
    text_logits = LOGIT_SCALE * jnp.einsum(
        "pd,bd->pb", text_emb, image_all, preferred_element_type=jnp.float32
    )
    image_log_total = row_log_total(image_logits)
    text_log_total = row_log_total(text_logits)
    loss_part = (
        jnp.sum(image_log_total - jnp.sum(diagonal_pick * image_logits, axis=1))
        + jnp.sum(text_log_total - jnp.sum(diagonal_pick * text_logits, axis=1))
    ) / (2.0 * pair_total)
    text_soft = ((jnp.exp(text_logits - text_log_total[:, None]) - diagonal_pick) * 0.5).astype(
        jnp.bfloat16
    )
    grad_text = LOGIT_SCALE * jnp.einsum(
        "pb,bd->pd", text_soft, image_all, preferred_element_type=jnp.float32
    )
    log_totals = lax.all_gather(image_log_total, ("dp", "rep"), axis=0, tiled=True)
    column_soft = ((jnp.exp(text_logits - log_totals[None, :]) - diagonal_pick) * 0.5).astype(
        jnp.bfloat16
    )
    grad_text = grad_text + LOGIT_SCALE * jnp.einsum(
        "pb,bd->pd", column_soft, image_all, preferred_element_type=jnp.float32
    )
    grad_pooled = embed_back(grad_text)[0].reshape(-1, PER_ROW, D) / counts
    grad_out = jnp.einsum("rks,rkd->rsd", caption_marks, grad_pooled, precision=PRECISE)
    grad_inputs, vector_grad, outer_terms = block_backward(
        text_float, allowed, text_low, vector_pieces, forward_kept, grad_out
    )
    blocks = [
        jnp.einsum("tc,tk->ck", left_side, right_side, preferred_element_type=jnp.float32)
        for left_side, right_side in outer_terms
    ]
    grad_rows = lax.psum_scatter(
        jnp.concatenate(blocks, axis=1), "dp", scatter_dimension=0, tiled=True
    )
    feedback_rows = error_feedback[0]
    worker_rows = grad_rows + feedback_rows
    factor_rows = jnp.concatenate(
        [
            rows_factor(start_factors[:, first_col:after_col], worker_rows[:, first_col:after_col])
            for first_col, after_col in bounds
        ],
        axis=0,
    )
    gathered_rows = lax.all_gather(factor_rows, "dp", axis=1, tiled=True)
    factor = lax.psum(gathered_rows.astype(jnp.bfloat16), "rep").astype(jnp.float32)
    vector_total, loss_total = lax.psum((vector_grad, loss_part), ("dp", "rep"))
    left_basis = orthonormal(factor.reshape(4, factor_rank, D)).reshape(4 * factor_rank, D)
    basis_rows = lax.dynamic_slice_in_dim(left_basis, row_start, own_rows, 1)
    right_part = jnp.concatenate(
        [
            jnp.einsum(
                "kd,dc->kc",
                basis_rows[matrix_id * factor_rank : (matrix_id + 1) * factor_rank],
                worker_rows[:, bounds[matrix_id][0] : bounds[matrix_id][1]],
                precision=PRECISE,
            )
            for matrix_id in range(4)
        ],
        axis=1,
    )
    new_right = lax.psum(right_part, ("dp", "rep"))
    approximation = jnp.concatenate(
        [
            jnp.einsum(
                "kd,kc->dc",
                basis_rows[matrix_id * factor_rank : (matrix_id + 1) * factor_rank],
                new_right[:, bounds[matrix_id][0] : bounds[matrix_id][1]],
                precision=PRECISE,
            )
            for matrix_id in range(4)
        ],
        axis=1,
    )
    new_feedback = (worker_rows - approximation / rep_count)[None]
    new_momentum = MOMENTUM_DECAY * momentum + approximation
    new_weights = text_weights - STEP_RATE * new_momentum
    new_vector_momentum = MOMENTUM_DECAY * vector_momentum + vector_total
    new_vectors = text_vectors - STEP_RATE * new_vector_momentum
    return (
        loss_total,
        text_output,
        grad_inputs,
        new_weights,
        new_momentum,
        new_feedback,
        new_vectors,
        new_vector_momentum,
        left_basis,
        new_right,
    )


def solution(mesh):
    placed = (
        P(("dp", "rep"), None, None),
        P("dp", None),
        P(),
        P(("dp", "rep"), None, None),
        P(("dp", "rep"), None),
        P("dp", None),
        P(),
        P("dp", None),
        P(),
        P("rep", "dp", None),
        P(),
    )
    return jax.shard_map(
        per_device,
        mesh=mesh,
        in_specs=placed,
        out_specs=(
            P(),
            P(("dp", "rep"), None, None),
            P(("dp", "rep"), None, None),
            P("dp", None),
            P("dp", None),
            P("rep", "dp", None),
            P(),
            P(),
            P(),
            P(),
        ),
        check_vma=False,
    )
```

profile of v0, /device:TPU:8, one launch (start us, length us, event | category | flops | bytes accessed | tf_op | source)
XLA Modules:
  0.0 1259.0 jit_solution(4314769996404762950)
XLA Ops:
  8.0 3.5 convert_element_type.126
  14.4 190.8 %all-gather.4.cloned.1.call-done = bf16[768,9216]{1,0:T(8,128)(2,1)} async-done(((bf16[96,9216]{1,0:T(8,128)(2,1)}), bf16[768,9216]{1,0:T(8,128)(2,1)}) %all-gather.4.cloned.1.call-update) | async-done | bytes 14155792 | tf_op jit(solution)/shard_map/all_gather | solution.py:272
  205.2 5.4 fusion.11
  210.5 5.9 reshape.907
  216.4 4.0 fusion.234
  223.5 1.5 reshape.906
  225.0 2.1 fusion.238
  227.4 6.5 fusion.72
  233.9 17.2 %fusion.76 = f32[8,768]{1,0:T(8,128)S(1)} fusion(f32[8,50,768]{2,1,0:T(8,128)S(1)} %get-tuple-element.130, bf16[768,9216]{1,0:T(8,128)(2,1)} %all-gather.4.cloned.1.call-done, f32[8,50,3072]{2,1,0:T(8,128)S(1)} %get-tuple-element.131, f32[3072]{0:T(1024)S(1)} %slice.199, u8[50,3072]{1,0:T(8,128)(4,1)S(1)} %get-tuple-element.11, ...), kind=kOutput, calls=%fused_computation.137 | convolution fusion | flops 1975597056 | bytes 11209728 | tf_op jit(solution)/shard_map/rsf,df->rsd/dot_general | solution.py:109
  251.9 149.9 %all-gather.6.cloned.1.call-done = bf16[768,9216]{1,0:T(8,128)(2,1)} async-done(((bf16[96,9216]{1,0:T(8,128)(2,1)}), bf16[768,9216]{1,0:T(8,128)(2,1)}) %all-gather.6.cloned.1.call-update) | async-done | bytes 14155792 | tf_op jit(solution)/shard_map/all_gather | solution.py:271
  401.8 2.7 fusion.12
  404.5 1.0 reshape.882
  405.5 1.1 fusion.235
  407.0 1.4 fusion.239
  408.9 1.7 fusion.240
  410.8 3.7 fusion.130
  414.7 1.1 copy-done.10
  415.8 4.4 multiply_convert_fusion
  420.2 4.3 fusion.84
  425.2 35.1 %all_gather.20 = bf16[256,768]{1,0:T(8,128)(2,1)S(1)} all-gather(bf16[8,768]{1,0:T(8,128)(2,1)S(1)} %multiply_convert_fusion.2), channel_id=1, replica_groups=mesh['dp'=8,'rep'=4] {'dp','rep'}, dimensions={0}, use_global_device_ids=true | all-gather | bytes 405504 | tf_op jit(solution)/shard_map/all_gather | solution.py:294
  460.3 37.8 %all_gather.21 = bf16[256,768]{1,0:T(8,128)(2,1)S(1)} all-gather(bf16[8,768]{1,0:T(8,128)(2,1)S(1)} %copy-done.23), channel_id=1, replica_groups=mesh['dp'=8,'rep'=4] {'dp','rep'}, dimensions={0}, use_global_device_ids=true | all-gather | bytes 405504 | tf_op jit(solution)/shard_map/all_gather | solution.py:293
  500.7 44.9 %all-reduce = f32[256]{0:T(256)S(1)} all-reduce(f32[256]{0:T(256)S(1)} %get-tuple-element.123), channel_id=1, replica_groups=mesh['dp'=8,'rep'=4] {'dp','rep'}, use_global_device_ids=true, to_apply=%add | all-reduce | flops 256 | bytes 2048
  546.5 5.3 convert_reduce_fusion.1
  551.8 5.0 multiply_reduce_fusion.3
  557.8 1.8 convolution_convert_fusion.3
  561.8 5.0 convolution_bitcast_fusion
  566.9 5.1 convolution_bitcast_fusion.1
  572.8 2.0 copy.270
  574.8 2.2 convert_element_type.144
  577.0 4.1 convolution_bitcast_fusion.2
  581.1 19.5 %pad_maximum_fusion = f32[768,9216]{1,0:T(8,128)} fusion(f32[768,3072]{1,0:T(8,128)} %convolution_bitcast_fusion, f32[768,3072]{1,0:T(8,128)} %convolution_bitcast_fusion.1, f32[768,768]{1,0:T(8,128)S(1)} %convolution_bitcast_fusion.3, f32[768,2304]{1,0:T(8,128)} %convolution_bitcast_fusion.2), kind=kLoop, calls=%fused_computation | loop fusion | flops 21233664 | bytes 56623104 | tf_op jit(solution)/shard_map/concatenate | solution.py:336
  602.2 3.4 fusion.230
  607.2 45.5 %all-reduce.1 = (f32[]{:T(128)}, f32[9216]{0:T(1024)}) all-reduce(f32[]{:T(128)S(6)} %div.223, f32[9216]{0:T(1024)S(1)} %constant_dynamic-update-slice_fusion.9), channel_id=1, replica_groups=mesh['dp'=8,'rep'=4] {'dp','rep'}, use_global_device_ids=true, to_apply=%region_24.25 | all-reduce | flops 9217 | bytes 73736 | tf_op jit(solution)/shard_map/psum | solution.py:349
  652.7 395.9 %reduce-scatter.2.cloned.1.call-done = f32[96,9216]{1,0:T(8,128)} async-done(((f32[768,9216]{1,0:T(8,128)}), f32[96,9216]{1,0:T(8,128)}) %reduce-scatter.2.cloned.1.call-update) | async-done | bytes 3538960 | tf_op jit(solution)/shard_map/reduce_scatter | solution.py:335
  1048.6 3.5 bitcast_add_fusion
  1052.1 1.0 fusion.96
  1053.1 1.0 fusion.93
  1055.3 29.7 %all-gather = bf16[8,96,32]{1,2,0:T(8,128)(2,1)S(1)} all-gather(bf16[1,96,32]{1,2,0:T(8,128)(2,1)S(1)} %maximum_bitcast_fusion), channel_id=1, replica_groups=mesh['dp'=8,'rep'=4] {'dp'}, dimensions={0}, use_global_device_ids=true | all-gather | bytes 55296 | tf_op jit(solution)/shard_map/all_gather | solution.py:347
  1085.7 1.6 reshape.893
  1087.3 1.4 copy.274
  1088.7 11.6 psum.29
  1108.3 1.4 multiply_subtract_fusion.1
  1109.8 128.2 %all-reduce.4.cloned.1.call-done = f32[8,9216]{1,0:T(8,128)} async-done(((f32[8,9216]{1,0:T(8,128)}), f32[8,9216]{1,0:T(8,128)}) %all-reduce.4.cloned.1.call-update) | async-done | bytes 294928 | tf_op jit(solution)/shard_map/psum | solution.py:364
  1238.0 2.2 fusion.138
  1240.2 2.1 fusion.140
  1242.3 1.3 fusion.151
  1243.6 1.9 fusion.146
  1245.5 6.1 multiply_subtract_fusion
  (239 shorter events, 28.8 us)
Async XLA Ops:
  7.2 198.0 %all-gather.4.cloned.1.call-start = ((), (), s32[]{:S(2)}) async-start(), calls=%async_computation.1 | async-start | bytes 15925248 | tf_op jit(solution)/shard_map/all_gather | solution.py:272
  7.9 3.7 copy-start.28
  7.9 4.2 copy-start.36
  7.9 4.9 copy-start.18
  7.9 5.5 copy-start.1
  8.0 5.8 copy-start.6
  8.0 393.8 %all-gather.6.cloned.1.call-start = ((), (), s32[]{:S(2)}) async-start(), calls=%async_computation.2 | async-start | bytes 15925248 | tf_op jit(solution)/shard_map/all_gather | solution.py:271
  11.5 1037.0 %reduce-scatter.2.cloned.1.call-start = ((), (), s32[]{:S(2)}) async-start(), calls=%async_computation.3 | async-start | bytes 31850496 | tf_op jit(solution)/shard_map/reduce_scatter | solution.py:335
  13.4 388.4 %copy-start.16 = (f32[768]{0:T(1024)}, f32[768]{0:T(1024)S(1)}, u32[]{:S(2)}) copy-start(f32[768]{0:T(1024)S(1)} %get-tuple-element.112) | copy-start | bytes 9220
  13.4 388.4 %copy-start.24 = (f32[768]{0:T(1024)}, f32[768]{0:T(1024)S(1)}, u32[]{:S(2)}) copy-start(f32[768]{0:T(1024)S(1)} %get-tuple-element.111) | copy-start | bytes 9220
  13.5 388.2 %copy-start.29 = (f32[2,64]{1,0:T(2,128)}, f32[2,64]{1,0:T(2,128)S(1)}, u32[]{:S(2)}) copy-start(f32[2,64]{1,0:T(2,128)S(1)} %broadcast_multiply_fusion.3) | copy-start | bytes 1540
  13.8 196.8 %copy-start.46 = (f32[2,64]{1,0:T(2,128)}, f32[2,64]{1,0:T(2,128)S(1)}, u32[]{:S(2)}) copy-start(f32[2,64]{1,0:T(2,128)S(1)} %fusion.124) | copy-start | bytes 1540
  14.3 387.5 %copy-start.31 = (f32[2,64]{1,0:T(2,128)}, f32[2,64]{1,0:T(2,128)S(1)}, u32[]{:S(2)}) copy-start(f32[2,64]{1,0:T(2,128)S(1)} %fusion.189) | copy-start | bytes 1540
  408.4 2.5 slice-start
  410.6 4.0 copy-start.33
  410.8 3.8 copy-start.48
  410.8 3.8 copy-start.38
  414.6 5.6 copy-start.50
  420.2 4.4 copy-start.4
  420.2 4.4 copy-start.37
  420.2 4.4 copy-start.43
  420.2 40.1 %copy-start.23 = (bf16[8,768]{1,0:T(8,128)(2,1)S(1)}, bf16[8,768]{1,0:T(8,128)(2,1)}, u32[]{:S(2)}) copy-start(bf16[8,768]{1,0:T(8,128)(2,1)} %multiply_convert_fusion.3) | copy-start | bytes 36868
  420.2 78.6 %copy-start.53 = (s32[8]{0:T(128)S(1)}, s32[8]{0:T(128)}, u32[]{:S(2)}) copy-start(s32[8]{0:T(128)} %iota_add_fusion) | copy-start | bytes 100
  424.6 121.4 %copy-start.14 = (f32[2,64,768]{2,1,0:T(8,128)}, f32[2,64,768]{2,1,0:T(8,128)S(1)}, u32[]{:S(2)}) copy-start(f32[2,64,768]{2,1,0:T(8,128)S(1)} %fusion.84) | copy-start | bytes 1179652
  546.4 5.3 copy-start.21
  546.4 5.3 copy-start.34
  546.5 5.3 copy-start.39
  551.8 5.0 copy-start.12
  551.8 5.0 copy-start.49
  561.8 5.1 copy-start.13
  561.8 5.1 copy-start.22
  561.8 5.1 copy-start.27
  561.8 5.1 copy-start.35
  561.8 5.1 copy-start.40
  572.8 4.2 copy-start.17
  572.8 4.2 copy-start.25
  572.8 4.2 copy-start.30
  572.8 4.2 copy-start.32
  600.6 637.4 %all-reduce.4.cloned.1.call-start = ((), (), s32[]{:S(2)}) async-start(), calls=%async_computation.4 | async-start | bytes 589824 | tf_op jit(solution)/shard_map/psum | solution.py:364
  602.2 3.5 copy-start.47
  602.2 3.9 copy-start.41
  602.2 3.9 copy-start.52
  602.2 4.0 copy-start.51
  602.2 4.0 copy-start.3
  602.2 4.0 copy-start.45
  1048.6 3.5 copy-start.15
  1238.0 7.5 copy-start
  1245.5 6.1 copy-start.11
  (11 other events, 16.4 us)
Sparse Core Ops, SparseCore 0:
  10.2 194.9 all-gather.3
  207.9 193.7 all-gather.5
  600.7 447.8 reduce-scatter.1
  1108.4 129.5 all-reduce.3
where the time goes:
time: 1270 us; the launch traced here: 1260 us
  waiting for transfers between devices  865 us (68%)
  blocking collectives  205 us (16%)
  matrix products  93.6 us (7%)
  other arithmetic  53.1 us (4%)
  local copies, waits for them, and re-layouts  25.4 us (2%)
  between operations  16.5 us (1%)
    reduce_scatter x1, waiting for transfers between devices, per_device(): lax.psum_scatter(jnp.concatenate(blocks, axis=1), 'dp', scatter_dimension...  396 us
    all_gather x1, waiting for transfers between devices, per_device(): lax.all_gather(image_weights, 'dp', axis=0, tiled=True)  191 us
    all_gather x1, waiting for transfers between devices, per_device(): lax.all_gather(text_weights.astype(jnp.bfloat16), 'dp', axis=0, tiled=True)  150 us
    psum x1, waiting for transfers between devices, per_device(): new_right = lax.psum(right_part, ('dp', 'rep'))  128 us
    psum x1, blocking collectives, per_device(): vector_total, loss_total = lax.psum((vector_grad, loss_part), ('dp', 'rep'))  45.5 us
    unnamed x1, blocking collectives  44.9 us
    all_gather x1, blocking collectives, per_device(): lax.all_gather(image_emb, ('dp', 'rep'), axis=0, tiled=True)  37.8 us
    all_gather x1, blocking collectives, per_device(): lax.all_gather(text_emb, ('dp', 'rep'), axis=0, tiled=True)  35.1 us
  transfers between devices with their start and end apart: 4, of which 4 were waited for; matrix products, arithmetic and copies ran while one was open for 5% of the time, Pallas kernels for 0%

commit v1 on v0

v1 whole, which is shorter than its diff:
```python
import functools

import jax
import jax.numpy as jnp
from jax import lax
from jax.experimental import pallas as pl
from jax.experimental.pallas import tpu as pltpu
from jax.sharding import PartitionSpec as P

D = 768
FF = 3072
HEADS = 12
HEAD_DIM = 64
PER_ROW = 4
GROUP = 4
SECTION = 3072
LANE_COLS = 512

PRECISE = lax.Precision.HIGHEST
LAYER_EPS = 1e-06
SCORE_SCALE = 0.125
LOGIT_SCALE = 50.0
MOMENTUM_DECAY = 0.9
STEP_RATE = 0.08
NORM_FLOOR = 1e-08
MASKED = -1e30
MESH = pl.DeviceIdType.MESH


def layer_norm(values, layer_gain, layer_shift):
    center = values - jnp.mean(values, axis=-1, keepdims=True)
    spread = jnp.mean(center * center, axis=-1, keepdims=True)
    return center * lax.rsqrt(spread + LAYER_EPS) * layer_gain + layer_shift


def unit_rows(values):
    return values * lax.rsqrt(jnp.sum(values * values, axis=-1, keepdims=True) + LAYER_EPS)


def vector_parts(vectors):
    pieces = [vectors[position * D : (position + 1) * D] for position in range(8)]
    return pieces + [vectors[8 * D :]]


def matrix_bounds():
    return ((0, 3 * D), (3 * D, 4 * D), (4 * D, 4 * D + FF), (4 * D + FF, 4 * D + 2 * FF))


def gather_kernel(
    n_dp, text_ref, image_ref, tok_ref, seg_ref, wt_ref, wi_ref, tok_out, seg_out,
    z_send, z_recv, y_send, y_recv, x_send, x_recv, c_send, c_recv, t_send, t_recv, t_own, own_sem,
):
    n_inner = n_dp // GROUP
    d_at, r_at = lax.axis_index("dp"), lax.axis_index("rep")
    z_at, y_at = d_at // n_inner, d_at % n_inner
    x_at, c_at = r_at // 2, r_at % 2
    z_peers = [(lax.rem(z_at + k, GROUP) * n_inner + y_at, r_at) for k in range(1, GROUP)]
    z_from = [lax.rem(z_at + GROUP - k, GROUP) for k in range(1, GROUP)]
    y_peers = [(z_at * n_inner + lax.rem(y_at + k, n_inner), r_at) for k in range(1, n_inner)]
    y_from = [lax.rem(y_at + n_inner - k, n_inner) for k in range(1, n_inner)]
    x_peer = (d_at, (1 - x_at) * 2 + c_at)
    c_peer = (d_at, x_at * 2 + 1 - c_at)

    barrier = pltpu.get_barrier_semaphore()
    everyone = z_peers + y_peers + [x_peer, c_peer]
    for peer in everyone:
        pl.semaphore_signal(barrier, inc=1, device_id=peer, device_id_type=MESH)
    pl.semaphore_wait(barrier, len(everyone))

    def shard_of(z, y):
        return z * n_inner + y

    sections = [(image_ref, wi_ref, 0), (text_ref, wt_ref, 0), (image_ref, wi_ref, 1),
                (text_ref, wt_ref, 1), (image_ref, wi_ref, 2), (text_ref, wt_ref, 2)]

    def cols(section, lane):
        start = sections[section][2] * SECTION + lane * LANE_COLS
        return pl.ds(pl.multiple_of(start, 128), LANE_COLS)

    lane_both = c_at
    lane_mine = 2 + x_at * 2 + c_at
    lane_theirs = 2 + (1 - x_at) * 2 + c_at
    lanes = (lane_both, lane_mine)

    locals_ = [
        pltpu.make_async_copy(tok_ref, tok_out.at[z_at], t_own.at[0]),
        pltpu.make_async_copy(seg_ref, seg_out.at[z_at], t_own.at[1]),
    ]
    for s, (src, full, _) in enumerate(sections):
        for j in range(2):
            column = cols(s, lanes[j])
            locals_.append(pltpu.make_async_copy(src.at[:, column], full.at[d_at, :, column], own_sem.at[s, j]))
    for copy in locals_:
        copy.start()

    def remote(src, dst, send, recv, peer):
        return pltpu.make_async_remote_copy(
            src_ref=src, dst_ref=dst, send_sem=send, recv_sem=recv, device_id=peer, device_id_type=MESH
        )

    def z_copy(s, k, j):
        src, full, _ = sections[s]
        return remote(
            src.at[:, cols(s, lanes[j])], full.at[d_at, :, cols(s, lanes[j])],
            z_send.at[s, k, j], z_recv.at[s, k, j], z_peers[k],
        )

    def y_copy(s, q, zi, j):
        src, full, _ = sections[s]
        column = cols(s, lanes[j])
        if zi == 0:
            shard, source = d_at, src.at[:, column]
        else:
            shard = shard_of(z_from[zi - 1], y_at)
            source = full.at[shard, :, column]
        return remote(source, full.at[shard, :, column], y_send.at[s, q, zi, j], y_recv.at[s, q, zi, j], y_peers[q])

    def x_copy(s):
        full = sections[s][1]
        block = full.at[:, :, cols(s, lane_mine)]
        return remote(block, block, x_send.at[s], x_recv.at[s], x_peer)

    def c_copy(s, j):
        full = sections[s][1]
        block = full.at[:, :, cols(s, (lane_both, lane_mine, lane_theirs)[j])]
        return remote(block, block, c_send.at[s, j], c_recv.at[s, j], c_peer)

    count = len(sections)
    tokens = []
    for k in range(GROUP - 1):
        tokens.append(remote(tok_ref, tok_out.at[z_at], t_send.at[0, k], t_recv.at[0, k], z_peers[k]))
        tokens.append(remote(seg_ref, seg_out.at[z_at], t_send.at[1, k], t_recv.at[1, k], z_peers[k]))

    def begin(s):
        for j in range(2):
            for k in range(GROUP - 1):
                z_copy(s, k, j).start()
            for q in range(n_inner - 1):
                y_copy(s, q, 0, j).start()

    begin(0)
    for copy in tokens:
        copy.start()
    for copy in locals_:
        copy.wait()
    begin(1)
    for step in range(count + 3):
        if step < count:
            for k in range(GROUP - 1):
                for j in range(2):
                    z_copy(step, k, j).wait_recv()
                    for q in range(n_inner - 1):
                        y_copy(step, q, k + 1, j).start()
            if step + 2 < count:
                begin(step + 2)
        s = step - 1
        if 0 <= s < count:
            for q in range(n_inner - 1):
                for zi in range(GROUP):
                    for j in range(2):
                        y_copy(s, q, zi, j).wait_recv()
            x_copy(s).start()
            for j in range(2):
                c_copy(s, j).start()
        s = step - 2
        if 0 <= s < count:
            x_copy(s).wait_recv()
            c_copy(s, 2).start()
        s = step - 3
        if 0 <= s < count:
            for j in range(3):
                c_copy(s, j).wait_recv()
    for copy in tokens:
        copy.wait()
    for s in range(count):
        for j in range(2):
            for k in range(GROUP - 1):
                z_copy(s, k, j).wait_send()
            for q in range(n_inner - 1):
                for zi in range(GROUP):
                    y_copy(s, q, zi, j).wait_send()
        x_copy(s).wait_send()
        for j in range(3):
            c_copy(s, j).wait_send()


def gather_weights(n_dp, text_low, image_low, tokens, segments):
    n_inner = n_dp // GROUP
    full = jax.ShapeDtypeStruct((n_dp,) + text_low.shape, jnp.bfloat16)
    hbm = pl.BlockSpec(memory_space=pltpu.HBM)
    dma = pltpu.SemaphoreType.DMA
    return pl.pallas_call(
        functools.partial(gather_kernel, n_dp),
        out_shape=(
            full,
            full,
            jax.ShapeDtypeStruct((GROUP,) + tokens.shape, jnp.bfloat16),
            jax.ShapeDtypeStruct((GROUP,) + segments.shape, jnp.int32),
        ),
        in_specs=[hbm] * 4,
        out_specs=(hbm,) * 4,
        scratch_shapes=[
            dma((6, GROUP - 1, 2)), dma((6, GROUP - 1, 2)),
            dma((6, n_inner - 1, GROUP, 2)), dma((6, n_inner - 1, GROUP, 2)),
            dma((6,)), dma((6,)), dma((6, 3)), dma((6, 3)),
            dma((2, GROUP - 1)), dma((2, GROUP - 1)), dma((2,)), dma((6, 2)),
        ],
        compiler_params=pltpu.CompilerParams(collective_id=1, has_side_effects=True),
        name="gather_weights",
    )(text_low, image_low, tokens, segments)


def peer_at(offset, n_dp, n_rep):
    me = lax.axis_index("dp") * n_rep + lax.axis_index("rep")
    other = lax.rem(me + offset, n_dp * n_rep)
    return other, (other // n_rep, lax.rem(other, n_rep))


def meet(n_dp, n_rep):
    total = n_dp * n_rep
    barrier = pltpu.get_barrier_semaphore()

    def hello(offset, carry):
        _, peer = peer_at(offset, n_dp, n_rep)
        pl.semaphore_signal(barrier, inc=1, device_id=peer, device_id_type=MESH)
        return carry

    lax.fori_loop(1, total, hello, 0)
    pl.semaphore_wait(barrier, total - 1)


def spread_kernel(n_dp, n_rep, mine_ref, all_ref, send, recv, own_sem):
    total = n_dp * n_rep
    me = lax.axis_index("dp") * n_rep + lax.axis_index("rep")
    own = pltpu.make_async_copy(mine_ref, all_ref.at[me], own_sem)
    own.start()
    meet(n_dp, n_rep)

    def copy(offset):
        _, peer = peer_at(offset, n_dp, n_rep)
        return pltpu.make_async_remote_copy(
            src_ref=mine_ref, dst_ref=all_ref.at[me], send_sem=send.at[offset - 1],
            recv_sem=recv.at[offset - 1], device_id=peer, device_id_type=MESH,
        )

    def begin(offset, carry):
        copy(offset).start()
        return carry

    def finish(offset, carry):
        copy(offset).wait()
        return carry

    lax.fori_loop(1, total, begin, 0)
    own.wait()
    lax.fori_loop(1, total, finish, 0)


def spread(mine, n_dp, n_rep, collective, name):
    total = n_dp * n_rep
    vmem = pl.BlockSpec(memory_space=pltpu.VMEM)
    dma = pltpu.SemaphoreType.DMA
    return pl.pallas_call(
        functools.partial(spread_kernel, n_dp, n_rep),
        out_shape=jax.ShapeDtypeStruct((total,) + mine.shape, mine.dtype),
        in_specs=[vmem],
        out_specs=vmem,
        scratch_shapes=[dma((total - 1,)), dma((total - 1,)), dma],
        compiler_params=pltpu.CompilerParams(
            collective_id=collective, has_side_effects=True, vmem_limit_bytes=48 << 20
        ),
        name=name,
    )(mine)


def total_kernel(n_dp, n_rep, mine_ref, out_ref, parts, sums, send, recv, send_two, recv_two):
    total = n_dp * n_rep
    me = lax.axis_index("dp") * n_rep + lax.axis_index("rep")
    meet(n_dp, n_rep)

    def scatter(offset):
        other, peer = peer_at(offset, n_dp, n_rep)
        return pltpu.make_async_remote_copy(
            src_ref=mine_ref.at[other], dst_ref=parts.at[offset - 1], send_sem=send.at[offset - 1],
            recv_sem=recv.at[offset - 1], device_id=peer, device_id_type=MESH,
        )

    def share(offset):
        _, peer = peer_at(offset, n_dp, n_rep)
        return pltpu.make_async_remote_copy(
            src_ref=sums, dst_ref=out_ref.at[me], send_sem=send_two.at[offset - 1],
            recv_sem=recv_two.at[offset - 1], device_id=peer, device_id_type=MESH,
        )

    def start_scatter(offset, carry):
        scatter(offset).start()
        return carry

    def add(offset, carry):
        scatter(offset).wait_recv()
        return carry + parts[offset - 1]

    def start_share(offset, carry):
        share(offset).start()
        return carry

    def finish(offset, carry):
        scatter(offset).wait_send()
        share(offset).wait()
        return carry

    lax.fori_loop(1, total, start_scatter, 0)
    result = lax.fori_loop(1, total, add, mine_ref[me])
    sums[...] = result
    lax.fori_loop(1, total, start_share, 0)
    out_ref[me] = result
    lax.fori_loop(1, total, finish, 0)


def total_over_all(flat, n_dp, n_rep, collective, name):
    total = n_dp * n_rep
    count = flat.shape[0]
    chunk = -(-count // (total * 1024)) * 1024
    padded = jnp.pad(flat, (0, total * chunk - count)).reshape(total, chunk // 128, 128)
    vmem = pl.BlockSpec(memory_space=pltpu.VMEM)
    dma = pltpu.SemaphoreType.DMA
    summed = pl.pallas_call(
        functools.partial(total_kernel, n_dp, n_rep),
        out_shape=jax.ShapeDtypeStruct(padded.shape, padded.dtype),
        in_specs=[vmem],
        out_specs=vmem,
        scratch_shapes=[
            pltpu.VMEM((total - 1,) + padded.shape[1:], padded.dtype),
            pltpu.VMEM(padded.shape[1:], padded.dtype),
            dma((total - 1,)), dma((total - 1,)), dma((total - 1,)), dma((total - 1,)),
        ],
        compiler_params=pltpu.CompilerParams(
            collective_id=collective, has_side_effects=True, vmem_limit_bytes=48 << 20
        ),
        name=name,
    )(padded)
    return summed.reshape(-1)[:count]


def masked_scores(query_heads, key_heads, allowed):
    scores = (
        jnp.einsum("rshd,rthd->rhst", query_heads, key_heads, preferred_element_type=jnp.float32)
        * SCORE_SCALE
    )
    return jnp.where(allowed[:, None], scores, MASKED)


def block_forward(inputs, allowed, weights, vector_pieces, pooled_only):
    (
        gain_one, shift_one, bias_query, bias_value, bias_out,
        gain_two, shift_two, bias_shrink, bias_expand,
    ) = vector_pieces
    row_count, seq_tokens = (inputs.shape[0], inputs.shape[1])
    normed = layer_norm(inputs, gain_one, shift_one).astype(jnp.bfloat16)
    mixing = jnp.einsum("rsd,dc->rsc", normed, weights[:, : 3 * D], preferred_element_type=jnp.float32)
    mixing = mixing + jnp.concatenate([bias_query, jnp.zeros_like(bias_query), bias_value])
    head_parts = mixing.astype(jnp.bfloat16).reshape(row_count, seq_tokens, 3, HEADS, HEAD_DIM)
    query_heads, key_heads, value_heads = (head_parts[:, :, 0], head_parts[:, :, 1], head_parts[:, :, 2])
    scores = masked_scores(query_heads, key_heads, allowed)
    highest = jnp.max(scores, axis=-1, keepdims=True)
    log_total = highest + jnp.log(jnp.sum(jnp.exp(scores - highest), axis=-1, keepdims=True))
    attention = jnp.exp(scores - log_total).astype(jnp.bfloat16)
    mixed_heads = jnp.einsum("rhst,rthd->rshd", attention, value_heads, preferred_element_type=jnp.float32)
    mixed_heads = mixed_heads.reshape(row_count, seq_tokens, D).astype(jnp.bfloat16)
    attended = (
        jnp.einsum("rsd,de->rse", mixed_heads, weights[:, 3 * D : 4 * D], preferred_element_type=jnp.float32)
        + bias_out
    )
    middle = inputs + attended
    normed_two = layer_norm(middle, gain_two, shift_two).astype(jnp.bfloat16)
    hidden = (
        jnp.einsum("rsd,df->rsf", normed_two, weights[:, 4 * D : 4 * D + FF], preferred_element_type=jnp.float32)
        + bias_expand
    )
    active = jax.nn.gelu(hidden, approximate=False).astype(jnp.bfloat16)
    shrink = weights[:, 4 * D + FF :]
    if pooled_only:
        mean_active = jnp.mean(active.astype(jnp.float32), axis=1)
        high = mean_active.astype(jnp.bfloat16)
        rest = mean_active - high.astype(jnp.float32)
        low = rest.astype(jnp.bfloat16)
        lower = (rest - low.astype(jnp.float32)).astype(jnp.bfloat16)
        stacked = jnp.concatenate([high, low, lower], axis=0)
        shrunk = jnp.einsum("pf,df->pd", stacked, shrink, preferred_element_type=jnp.float32)
        shrunk = jnp.sum(shrunk.reshape(3, row_count, D), axis=0)
        return jnp.mean(middle, axis=1) + shrunk + bias_shrink
    shrunk = jnp.einsum("rsf,df->rsd", active, shrink, preferred_element_type=jnp.float32) + bias_shrink
    kept = (normed, query_heads, key_heads, value_heads, log_total, mixed_heads, middle, normed_two, hidden, active)
    return (middle + shrunk, kept)


def token_sum(values_low):
    return jnp.sum(values_low.astype(jnp.float32).reshape(-1, values_low.shape[-1]), axis=0)


def block_backward(inputs, allowed, weights, vector_pieces, forward_kept, grad_out, own_group, own_count):
    (gain_one, shift_one, _, _, _, gain_two, shift_two, _, _) = vector_pieces
    (normed, query_heads, key_heads, value_heads, log_total, mixed_heads, middle, normed_two, hidden, active) = forward_kept
    row_count, seq_tokens = (inputs.shape[0], inputs.shape[1])
    grad_shrunk = grad_out.astype(jnp.bfloat16)
    grad_active = jnp.einsum("rsd,df->rsf", grad_shrunk, weights[:, 4 * D + FF :], preferred_element_type=jnp.float32)
    _, gelu_back = jax.vjp(lambda before_gelu: jax.nn.gelu(before_gelu, approximate=False), hidden)
    grad_hidden = gelu_back(grad_active)[0].astype(jnp.bfloat16)
    grad_normed_two = jnp.einsum(
        "rsf,df->rsd", grad_hidden, weights[:, 4 * D : 4 * D + FF], preferred_element_type=jnp.float32
    )
    _, norm_two_back = jax.vjp(layer_norm, middle, gain_two, shift_two)
    grad_middle, grad_gain_two, grad_shift_two = norm_two_back(grad_normed_two)
    grad_middle = grad_middle + grad_out
    grad_attended = grad_middle.astype(jnp.bfloat16)
    grad_mixed = jnp.einsum("rse,de->rsd", grad_attended, weights[:, 3 * D : 4 * D], preferred_element_type=jnp.float32)
    grad_mixed = grad_mixed.astype(jnp.bfloat16).reshape(row_count, seq_tokens, HEADS, HEAD_DIM)
    attention = jnp.exp(masked_scores(query_heads, key_heads, allowed) - log_total)
    grad_values = jnp.einsum("rhst,rshd->rthd", attention.astype(jnp.bfloat16), grad_mixed, preferred_element_type=jnp.float32)
    grad_attention = jnp.einsum("rshd,rthd->rhst", grad_mixed, value_heads, preferred_element_type=jnp.float32)
    grad_scores = attention * (grad_attention - jnp.sum(attention * grad_attention, axis=-1, keepdims=True))
    grad_scores = grad_scores.astype(jnp.bfloat16)
    grad_query = jnp.einsum("rhst,rthd->rshd", grad_scores, key_heads, preferred_element_type=jnp.float32) * SCORE_SCALE
    grad_keys = jnp.einsum("rhst,rshd->rthd", grad_scores, query_heads, preferred_element_type=jnp.float32) * SCORE_SCALE
    grad_mixing = (
        jnp.stack([grad_query, grad_keys, grad_values], axis=2).reshape(row_count, seq_tokens, 3 * D).astype(jnp.bfloat16)
    )

    def mine(values):
        return lax.dynamic_slice_in_dim(values, own_group * own_count, own_count, 0)

    grad_normed = jnp.einsum("rsc,dc->rsd", mine(grad_mixing), weights[:, : 3 * D], preferred_element_type=jnp.float32)
    _, norm_one_back = jax.vjp(layer_norm, mine(inputs), gain_one, shift_one)
    grad_inputs, grad_gain_one, grad_shift_one = norm_one_back(grad_normed)
    grad_inputs = grad_inputs + mine(grad_middle)
    share = 1.0 / GROUP
    vector_grad = jnp.concatenate(
        [
            grad_gain_one, grad_shift_one,
            share * token_sum(grad_mixing[..., :D]), share * token_sum(grad_mixing[..., 2 * D :]),
            share * token_sum(grad_attended), share * grad_gain_two, share * grad_shift_two,
            share * token_sum(grad_shrunk), share * token_sum(grad_hidden),
        ]
    )
    tokens = row_count * seq_tokens
    outer_terms = (
        (normed.reshape(tokens, D), grad_mixing.reshape(tokens, 3 * D)),
        (mixed_heads.reshape(tokens, D), grad_attended.reshape(tokens, D)),
        (normed_two.reshape(tokens, D), grad_hidden.reshape(tokens, FF)),
        (grad_shrunk.reshape(tokens, D), active.reshape(tokens, FF)),
    )
    return (grad_inputs, vector_grad, outer_terms)


def orthonormal(stacked):
    waiting = [stacked[:, column_id] for column_id in range(stacked.shape[1])]
    finished = []
    while waiting:
        vector = waiting.pop(0)
        vector = vector / (jnp.sqrt(jnp.sum(vector * vector, axis=-1, keepdims=True)) + NORM_FLOOR)
        finished.append(vector)
        if waiting:
            later = jnp.stack(waiting, axis=1)
            later = later - jnp.sum(vector[:, None] * later, axis=-1, keepdims=True) * vector[:, None]
            waiting = [later[:, i] for i in range(later.shape[1])]
    return jnp.stack(finished, axis=1)


def rows_factor(start_part, row_block):
    return jnp.einsum("kc,dc->kd", start_part, row_block, precision=PRECISE)


def per_device(
    image_tokens, image_weights, image_vectors, text_tokens, segments, text_weights,
    text_vectors, momentum, vector_momentum, error_feedback, start_factors,
):
    n_rep, n_dp = lax.axis_size("rep"), lax.axis_size("dp")
    n_inner = n_dp // GROUP
    total = n_rep * n_dp
    device_pairs, patches = image_tokens.shape[0], image_tokens.shape[1]
    text_rows, seq_tokens = text_tokens.shape[0], text_tokens.shape[1]
    pair_total = device_pairs * total
    own_rows = text_weights.shape[0]
    d_at, r_at = lax.axis_index("dp"), lax.axis_index("rep")
    z_at, y_at = d_at // n_inner, d_at % n_inner
    row_start = d_at * own_rows
    factor_rank = start_factors.shape[0]
    bounds = matrix_bounds()
    text_low, frozen, token_group, segment_group = gather_weights(
        n_dp, text_weights.astype(jnp.bfloat16), image_weights,
        text_tokens.reshape(text_rows * seq_tokens, D), segments,
    )
    text_low, frozen = text_low.reshape(D, -1), frozen.reshape(D, -1)
    full_mask = jnp.zeros((device_pairs, patches, patches), jnp.int32) == 0
    image_pooled = block_forward(
        image_tokens.astype(jnp.float32), full_mask, frozen, vector_parts(image_vectors), True
    )
    image_emb = unit_rows(image_pooled).astype(jnp.bfloat16)

    group_rows = GROUP * text_rows
    text_float = token_group.reshape(group_rows, seq_tokens, D).astype(jnp.float32)
    segment_all = segment_group.reshape(group_rows, seq_tokens)
    allowed = segment_all[:, :, None] == segment_all[:, None, :]
    vector_pieces = vector_parts(text_vectors)
    group_output, forward_kept = block_forward(text_float, allowed, text_low, vector_pieces, False)
    text_output = lax.dynamic_slice_in_dim(group_output, z_at * text_rows, text_rows, 0)
    caption_marks = (
        segment_all[:, None, :] == jnp.arange(PER_ROW, dtype=jnp.int32)[None, :, None]
    ).astype(jnp.float32)
    counts = jnp.sum(caption_marks, axis=-1, keepdims=True)
    pooled = (jnp.einsum("rks,rsd->rkd", caption_marks, group_output, precision=PRECISE) / counts).reshape(-1, D)
    text_norm, embed_back = jax.vjp(unit_rows, pooled)
    text_emb = text_norm.astype(jnp.bfloat16)
    own_emb = lax.dynamic_slice_in_dim(text_emb, z_at * device_pairs, device_pairs, 0)
    embeddings = spread(jnp.concatenate([image_emb, own_emb], axis=0), n_dp, n_rep, 2, "spread_embeddings")
    image_all = embeddings[:, :device_pairs].reshape(pair_total, D)
    text_all = embeddings[:, device_pairs:].reshape(pair_total, D)
    own_pairs = (
        ((jnp.arange(GROUP, dtype=jnp.int32) * n_inner + y_at) * n_rep + r_at)[:, None] * device_pairs
        + jnp.arange(device_pairs, dtype=jnp.int32)[None, :]
    ).reshape(-1)
    logits = LOGIT_SCALE * jnp.einsum("pd,bd->pb", image_all, text_all, preferred_element_type=jnp.float32)
    image_top = jnp.max(logits, axis=1)
    image_log_total = image_top + jnp.log(jnp.sum(jnp.exp(logits - image_top[:, None]), axis=1))
    caption_top = jnp.max(logits, axis=0)
    caption_log_total = caption_top + jnp.log(jnp.sum(jnp.exp(logits - caption_top[None, :]), axis=0))
    pair_ids = jnp.arange(pair_total, dtype=jnp.int32)
    matched = jnp.sum(jnp.where(pair_ids[:, None] == pair_ids[None, :], logits, 0.0), axis=1)
    loss_total = (jnp.sum(image_log_total - matched) + jnp.sum(caption_log_total - matched)) / (2.0 * pair_total)
    diagonal_pick = (pair_ids[None, :] == own_pairs[:, None]).astype(jnp.float32)
    text_logits = LOGIT_SCALE * jnp.einsum("pd,bd->pb", text_emb, image_all, preferred_element_type=jnp.float32)
    text_top = jnp.max(text_logits, axis=1, keepdims=True)
    text_log_total = text_top + jnp.log(jnp.sum(jnp.exp(text_logits - text_top), axis=1, keepdims=True))
    text_soft = ((jnp.exp(text_logits - text_log_total) - diagonal_pick) * 0.5).astype(jnp.bfloat16)
    column_soft = ((jnp.exp(text_logits - image_log_total[None, :]) - diagonal_pick) * 0.5).astype(jnp.bfloat16)
    grad_text = LOGIT_SCALE * (
        jnp.einsum("pb,bd->pd", text_soft, image_all, preferred_element_type=jnp.float32)
        + jnp.einsum("pb,bd->pd", column_soft, image_all, preferred_element_type=jnp.float32)
    )
    grad_pooled = embed_back(grad_text)[0].reshape(-1, PER_ROW, D) / counts
    grad_out = jnp.einsum("rks,rkd->rsd", caption_marks, grad_pooled, precision=PRECISE)
    grad_inputs, vector_grad, outer_terms = block_backward(
        text_float, allowed, text_low, vector_pieces, forward_kept, grad_out, z_at, text_rows
    )
    group_width = n_inner * own_rows
    worker_blocks = []
    feedback_rows = error_feedback[0]
    for (left_side, right_side), (first_col, after_col) in zip(outer_terms, bounds):
        left_cut = lax.dynamic_slice_in_dim(left_side, z_at * group_width, group_width, 1)
        block = jnp.einsum("tc,tk->ck", left_cut, right_side, preferred_element_type=jnp.float32)
        mine = lax.dynamic_slice_in_dim(block, y_at * own_rows, own_rows, 0)
        for k in range(1, n_inner):
            target = lax.rem(y_at + k, n_inner)
            outgoing = lax.dynamic_slice_in_dim(block, target * own_rows, own_rows, 0).astype(jnp.bfloat16)
            pairs = [
                (z * n_inner + y, z * n_inner + (y + k) % n_inner) for z in range(GROUP) for y in range(n_inner)
            ]
            mine = mine + lax.ppermute(outgoing, "dp", pairs).astype(jnp.float32)
        worker_blocks.append(mine + feedback_rows[:, first_col:after_col])
    factor_rows = jnp.concatenate(
        [
            rows_factor(start_factors[:, first_col:after_col], rows)
            for rows, (first_col, after_col) in zip(worker_blocks, bounds)
        ],
        axis=0,
    )
    gathered_rows = spread(factor_rows, n_dp, n_rep, 3, "spread_factors")
    factor = jnp.sum(gathered_rows.reshape(n_dp, n_rep, 4 * factor_rank, own_rows), axis=1)
    factor = jnp.swapaxes(factor, 0, 1).reshape(4, factor_rank, D)
    left_basis = orthonormal(factor).reshape(4 * factor_rank, D)
    basis_rows = lax.dynamic_slice_in_dim(left_basis, row_start, own_rows, 1)
    basis_parts = [basis_rows[i * factor_rank : (i + 1) * factor_rank] for i in range(4)]
    right_part = jnp.concatenate(
        [jnp.einsum("kd,dc->kc", part, rows, precision=PRECISE) for part, rows in zip(basis_parts, worker_blocks)],
        axis=1,
    )
    summed = total_over_all(
        jnp.concatenate([right_part.reshape(-1), vector_grad]), n_dp, n_rep, 4, "total_right"
    )
    new_right = summed[: right_part.size].reshape(right_part.shape)
    vector_total = summed[right_part.size :]
    approximation = jnp.concatenate(
        [
            jnp.einsum("kd,kc->dc", part, new_right[:, first_col:after_col], precision=PRECISE)
            for part, (first_col, after_col) in zip(basis_parts, bounds)
        ],
        axis=1,
    )
    worker_rows = jnp.concatenate(worker_blocks, axis=1)
    new_feedback = (worker_rows - approximation / n_rep)[None]
    new_momentum = MOMENTUM_DECAY * momentum + approximation
    new_weights = text_weights - STEP_RATE * new_momentum
    new_vector_momentum = MOMENTUM_DECAY * vector_momentum + vector_total
    new_vectors = text_vectors - STEP_RATE * new_vector_momentum
    return (
        loss_total, text_output, grad_inputs, new_weights, new_momentum, new_feedback,
        new_vectors, new_vector_momentum, left_basis, new_right,
    )


def solution(mesh):
    placed = (
        P(("dp", "rep"), None, None), P("dp", None), P(), P(("dp", "rep"), None, None), P(("dp", "rep"), None),
        P("dp", None), P(), P("dp", None), P(), P("rep", "dp", None), P(),
    )
    return jax.shard_map(
        per_device,
        mesh=mesh,
        in_specs=placed,
        out_specs=(
            P(), P(("dp", "rep"), None, None), P(("dp", "rep"), None, None), P("dp", None), P("dp", None),
            P("rep", "dp", None), P(), P(), P(), P(),
        ),
        check_vma=False,
    )
```

time: 1270 us -> 543 us (0.43)
  waiting for transfers between devices: 865 us -> 0.01 us
  Pallas kernels: 0 us -> 245 us
  blocking collectives: 205 us -> 0 us
  local copies, waits for them, and re-layouts: 25.4 us -> 98 us
  other arithmetic: 53.1 us -> 81.4 us
    reduce_scatter x1 -> x0, waiting for transfers between devices: 396 us -> none  [per_device(): lax.psum_scatter(jnp.concatenate(blocks, axis=1), 'dp', scatter_dimension...]
    all_gather x2 -> x0, waiting for transfers between devices: 341 us -> none  [the longest x1 191 us: per_device(): lax.all_gather(image_weights, 'dp', axis=0, tiled=True)]
    pallas_call x0 -> x4, Pallas kernels: none -> 245 us  [the longest x1 179 us: gather_weights(): pl.pallas_call(functools.partial(gather_kernel, n_dp), out_shape=(full, f...]
    psum x1 -> x0, waiting for transfers between devices: 128 us -> none  [per_device(): new_right = lax.psum(right_part, ('dp', 'rep'))]
    all_gather x3 -> x0, blocking collectives: 103 us -> none  [the longest x1 37.8 us: per_device(): lax.all_gather(image_emb, ('dp', 'rep'), axis=0, tiled=True)]
    psum x2 -> x0, blocking collectives: 57.1 us -> none  [the longest x1 45.5 us: per_device(): vector_total, loss_total = lax.psum((vector_grad, loss_part), ('dp', 'rep'))]
    unnamed x1 -> x0, blocking collectives: 44.9 us -> none
    convert_element_type x3 -> x9, local copies, waits for them, and re-layouts: 4.39 us -> 33.8 us  [the longest x4 31.2 us: block_backward(): jnp.stack([grad_query, grad_keys, grad_values], axis=2)]
  transfers between devices with their start and end apart: 4 -> 4, of which waited for: 4 -> 0; matrix products, arithmetic and copies ran while one was open for 5% -> 19% of each run, Pallas kernels for 0% -> 0%
where the time goes in v1:
time: 543 us; the launch traced here: 534 us
  Pallas kernels  245 us (45%)
  matrix products  100 us (18%)
  local copies, waits for them, and re-layouts  98 us (18%)
  other arithmetic  81.4 us (15%)
    pallas_call x1, Pallas kernels, gather_weights(): pl.pallas_call(functools.partial(gather_kernel, n_dp), out_shape=(full, f...  179 us
    pallas_call x2, Pallas kernels, spread(): pl.pallas_call(functools.partial(spread_kernel, n_dp, n_rep), out_shape=j...  41.4 us
    convert_element_type x4, local copies, waits for them, and re-layouts, block_backward(): jnp.stack([grad_query, grad_keys, grad_values], axis=2)  31.2 us
    pallas_call x1, Pallas kernels, total_over_all(): pl.pallas_call(functools.partial(total_kernel, n_dp, n_rep), out_shape=ja...  24.7 us
    convert_element_type x1, other arithmetic, block_forward(): active = jax.nn.gelu(hidden, approximate=False).astype(jnp.bfloat16)  15.3 us
    unnamed x139, local copies, waits for them, and re-layouts  14.5 us
    reshape x2, local copies, waits for them, and re-layouts, block_forward(): mixing.astype(jnp.bfloat16)  14.5 us
    reduce_sum x1, other arithmetic, block_forward(): mean_active = jnp.mean(active.astype(jnp.float32), axis=1)  12.9 us
  transfers between devices with their start and end apart: 4, of which 0 were waited for; matrix products, arithmetic and copies ran while one was open for 19% of the time, Pallas kernels for 0%

profile of v1, /device:TPU:8, one launch (start us, length us, event | category | flops | bytes accessed | tf_op | source)
XLA Modules:
  0.0 533.8 jit_solution(17652291464415918947)
XLA Ops:
  3.5 3.4 convert_element_type.188.text_ref
  7.0 179.3 %gather_weights.1 = (bf16[8,96,9216]{2,1,0:T(8,128)(2,1)}, bf16[8,96,9216]{2,1,0:T(8,128)(2,1)}, bf16[4,128,768]{2,1,0:T(8,128)(2,1)}, s32[4,2,64]{2,1,0:T(2,128)}) custom-call(bf16[96,9216]{1,0:T(8,128)(2,1)} %convert_element_type.188.text_ref, bf16[96,9216]{1,0:T(8,128)(2,1)} %image_ref.1, bf16[128,768]{1,0:T(8,128)(2,1)} %bitcast.237, s32[2,64]{1,0:T(2,128)} %seg_ref.1), custom_call_target="tpu_custom_call" | custom-call | tf_op jit(solution)/shard_map/gather_weights/pallas_call | solution.py:192
  194.8 5.4 %fusion.19 = bf16[8,50,2304]{2,1,0:T(8,128)(2,1)} fusion(bf16[768,9216]{1,0:T(8,128)(2,1)} %bitcast.274, f32[2304]{0:T(1024)S(1)} %get-tuple-element.85, f32[768]{0:T(1024)S(1)} %get-tuple-element.72, f32[768]{0:T(1024)S(1)} %get-tuple-element.73, f32[8,50]{1,0:T(8,128)S(1)} %add_rsqrt_fusion.1, f32[8,50]{1,0:T(8,128)S(1)} %broadcast_multiply_fusion.2, ...), kind=kOutput, calls=%fused_computation.52 | convolution fusion | flops 1419264000 | bytes 6015104 | tf_op jit(solution)/shard_map/rsd,dc->rsc/dot_general | solution.py:360
  200.2 6.3 %reshape.620 = bf16[8,50,3,12,64]{4,3,2,1,0:T(8,128)(2,1)} reshape(bf16[8,50,2304]{2,1,0:T(8,128)(2,1)} %fusion.19) | data formatting | bytes 3686400 | tf_op jit(solution)/shard_map/reshape | solution.py:362
  206.5 3.4 fusion.162
  214.8 2.4 fusion.166
  217.6 5.6 %fusion.18 = bf16[8,64,2304]{2,1,0:T(8,128)(2,1)} fusion(bf16[768,9216]{1,0:T(8,128)(2,1)} %bitcast.264, f32[2304]{0:T(1024)S(1)} %get-tuple-element.86, f32[8,64,768]{2,1,0:T(8,128)S(1)} %bitcast.210, f32[768]{0:T(1024)S(1)} %get-tuple-element.121, f32[768]{0:T(1024)S(1)} %get-tuple-element.120, f32[8,64]{1,0:T(8,128)S(1)} %rsqrt.77, f32[8,64]{1,0:T(8,128)S(1)} %div.191), kind=kOutput, calls=%fused_computation.51 | convolution fusion | flops 1816264704 | bytes 7490560 | tf_op jit(solution)/shard_map/rsd,dc->rsc/dot_general | solution.py:360
  223.3 8.1 %reshape.593 = bf16[8,64,3,12,64]{4,3,2,1,0:T(8,128)(2,1)} reshape(bf16[8,64,2304]{2,1,0:T(8,128)(2,1)} %fusion.18) | data formatting | bytes 4718592 | tf_op jit(solution)/shard_map/reshape | solution.py:362
  231.4 6.4 %fusion.161 = (bf16[8,64,1,12,64]{4,3,2,1,0:T(8,128)(2,1)}, bf16[8,64,1,12,64]{4,3,2,1,0:T(8,128)(2,1)S(1)}, bf16[8,64,1,12,64]{4,3,2,1,0:T(8,128)(2,1)}) fusion(bf16[8,64,3,12,64]{4,3,2,1,0:T(8,128)(2,1)} %reshape.593), kind=kLoop, calls=%fused_computation.367 | loop fusion | bytes 4718592 | tf_op jit(solution)/shard_map/slice | solution.py:363
  237.9 3.1 copy.149
  240.9 3.3 fusion.24
  247.0 2.4 fusion.165
  249.8 5.9 %fusion.41 = (u8[50,3072]{1,0:T(8,128)(4,1)S(1)}, f32[8,50,3072]{2,1,0:T(8,128)S(1)}) fusion(f32[3072]{0:T(1024)S(1)} %slice.254, bf16[768,9216]{1,0:T(8,128)(2,1)} %bitcast.276, f32[8,50,768]{2,1,0:T(8,128)S(1)} %copy-done.28, f32[768]{0:T(1024)S(1)} %get-tuple-element.68, f32[768]{0:T(1024)S(1)} %get-tuple-element.67, f32[8,50]{1,0:T(8,128)S(1)} %add_rsqrt_fusion, ...), kind=kOutput, calls=%fused_computation.119 | convolution fusion | flops 1899878400 | bytes 11037824 | tf_op jit(solution)/shard_map/rsd,df->rsf/dot_general | solution.py:377
  255.7 12.9 %convert_reduce_fusion.1 = f32[8,3072]{1,0:T(8,128)S(1)} fusion(f32[8,50,3072]{2,1,0:T(8,128)S(1)} %get-tuple-element.107, f32[3072]{0:T(1024)S(1)} %slice.254, u8[50,3072]{1,0:T(8,128)(4,1)S(1)} %get-tuple-element.106), kind=kLoop, calls=%fused_computation.29 | loop fusion | flops 87220224 | bytes 5179392 | tf_op jit(solution)/shard_map/reduce_sum | solution.py:383
  268.7 3.7 fusion.46
  273.5 4.3 fusion.32
  277.9 15.3 %multiply_convert_fusion = (bf16[8,64,3072]{2,1,0:T(8,128)(2,1)S(1)}, f32[8,64,3072]{2,1,0:T(8,128)}) fusion(f32[8,64,3072]{2,1,0:T(8,128)S(1)} %get-tuple-element.99, f32[3072]{0:T(1024)S(1)} %slice.270, u8[64,3072]{1,0:T(8,128)(4,1)S(1)} %get-tuple-element.19, u8[64,3072]{1,0:T(8,128)(4,1)S(1)} %get-tuple-element.18), kind=kLoop, calls=%fused_computation.11 | loop fusion | flops 111673344 | bytes 16134144 | tf_op jit(solution)/shard_map/convert_element_type | solution.py:380
  293.2 2.7 add_add_fusion.2
  300.6 23.7 %spread_embeddings.1 = bf16[32,16,768]{2,1,0:T(8,128)(2,1)S(1)} custom-call(bf16[16,768]{1,0:T(8,128)(2,1)S(1)} %pad_maximum_fusion.mine_ref), custom_call_target="tpu_custom_call" | custom-call | tf_op jit(solution)/shard_map/spread_embeddings/pallas_call | solution.py:263
  328.1 2.9 convert_reduce_fusion.3
  331.1 3.0 fusion.81
  336.4 1.9 collective-permute-start.3
  338.3 9.6 %convert_reduce_fusion = (f32[3072]{0:T(1024)}, bf16[8,64,3072]{2,1,0:T(8,128)(2,1)S(1)}) fusion(f32[8,64,3072]{2,1,0:T(8,128)} %get-tuple-element.55, bf16[8,64,768]{2,1,0:T(8,128)(2,1)S(1)} %copy-done.26, bf16[768,9216]{1,0:T(8,128)(2,1)} %bitcast.266, f32[8,64,3072]{2,1,0:T(8,128)} %copy-done.18, f32[3072]{0:T(1024)S(1)} %slice.270), kind=kOutput, calls=%fused_computation.9 | convolution fusion | flops 2442654720 | bytes 21258240 | tf_op jit(solution)/shard_map/rsd,df->rsf/dot_general | solution.py:406
  347.9 2.0 fusion.83
  352.4 6.8 %fusion.157 = (f32[768]{0:T(1024)}, f32[8,64]{1,0:T(8,128)S(1)}, f32[8,64,768]{2,1,0:T(8,128)}) fusion(f32[768]{0:T(1024)S(1)} %get-tuple-element.125, f32[8,64,768]{2,1,0:T(8,128)S(1)} %copy-done.1, f32[8,64]{1,0:T(8,128)S(1)} %broadcast_multiply_fusion, bf16[8,64,3072]{2,1,0:T(8,128)(2,1)S(1)} %get-tuple-element.119, bf16[768,9216]{1,0:T(8,128)(2,1)} %bitcast.267), kind=kOutput, calls=%fused_computation.364 | convolution fusion | flops 2417883904 | bytes 11020288 | tf_op jit(solution)/shard_map/rsf,df->rsd/dot_general | solution.py:409
  359.3 2.4 copy.122
  361.7 3.6 convert_element_type.234
  365.4 3.3 multiply_reduce_fusion.2
  368.7 3.8 convert_reduce_fusion.4
  377.9 3.0 convolution_convert_fusion.2
  380.8 2.4 copy.152
  383.3 2.5 convolution_bitcast_fusion
  391.2 2.7 maximum_convert_fusion
  393.9 7.0 %copy.121 = bf16[8,64,3,12,64]{1,0,4,3,2:T(8,128)(2,1)} copy(bf16[8,64,3,12,64]{4,1,3,0,2:T(8,128)(2,1)} %maximum_convert_fusion) | data formatting | bytes 4718592 | tf_op jit(solution)/shard_map/convert_element_type | solution.py:426
  400.9 7.7 %convert_element_type.231 = bf16[512,2304]{0,1:T(8,128)(2,1)} reshape(bf16[8,64,3,12,64]{1,0,4,3,2:T(8,128)(2,1)} %copy.121) | data formatting | bytes 4718592 | tf_op jit(solution)/shard_map/convert_element_type | solution.py:426
  408.6 3.0 fusion.75
  413.2 8.2 %copy.120 = bf16[8,64,3,12,64]{4,3,2,1,0:T(8,128)(2,1)} copy(bf16[8,64,3,12,64]{4,1,3,0,2:T(8,128)(2,1)} %maximum_convert_fusion) | data formatting | bytes 4718592 | tf_op jit(solution)/shard_map/convert_element_type | solution.py:426
  421.5 8.4 %convert_element_type.227 = bf16[8,64,2304]{2,1,0:T(8,128)(2,1)} reshape(bf16[8,64,3,12,64]{4,3,2,1,0:T(8,128)(2,1)} %copy.120) | data formatting | bytes 4718592 | tf_op jit(solution)/shard_map/convert_element_type | solution.py:426
  429.9 4.3 multiply_reduce_fusion.9
  435.0 1.9 dynamic-slice_add_fusion
  447.0 3.2 slice_add_fusion.1
  452.3 17.7 %spread_factors.1 = f32[32,32,96]{2,1,0:T(8,128)S(1)} custom-call(f32[32,96]{1,0:T(8,128)S(1)} %pad_maximum_fusion.3.mine_ref), custom_call_target="tpu_custom_call" | custom-call | tf_op jit(solution)/shard_map/spread_factors/pallas_call | solution.py:263
  489.5 24.7 %total_right.1 = f32[32,24,128]{2,1,0:T(8,128)S(1)} custom-call(f32[32,24,128]{2,1,0:T(8,128)S(1)} %bitcast.207), custom_call_target="tpu_custom_call" | custom-call | tf_op jit(solution)/shard_map/total_right/pallas_call | solution.py:327
  518.8 1.9 fusion.105
  520.7 2.1 fusion.99
  522.8 2.1 fusion.101
  525.5 4.8 multiply_subtract_fusion
  530.4 2.0 maximum_subtract_fusion
  (293 shorter events, 82.4 us)
Async XLA Ops:
  3.5 214.1 %copy-start.54 = (f32[768]{0:T(1024)}, f32[768]{0:T(1024)S(1)}, u32[]{:S(2)}) copy-start(f32[768]{0:T(1024)S(1)} %get-tuple-element.121) | copy-start | bytes 9220
  7.0 186.6 %copy-start.22 = (bf16[8,50,768]{2,0,1:T(8,128)(2,1)S(1)}, bf16[8,50,768]{2,0,1:T(8,128)(2,1)}, u32[]{:S(2)}) copy-start(bf16[8,50,768]{2,0,1:T(8,128)(2,1)} %param.11) | copy-start | bytes 1843204
  190.5 105.3 %copy-start.40 = (f32[8,4]{1,0:T(8,128)}, f32[8,4]{1,0:T(8,128)S(1)}, u32[]{:S(2)}) copy-start(f32[8,4]{1,0:T(8,128)S(1)} %convert_reduce_fusion.8) | copy-start | bytes 388
  192.7 24.9 %copy-start.3 = (f32[4,128,768]{2,1,0:T(8,128)}, f32[4,128,768]{2,1,0:T(8,128)S(1)}, u32[]{:S(2)}) copy-start(f32[4,128,768]{2,1,0:T(8,128)S(1)} %convert_element_type.246) | copy-start | bytes 4718596
  217.2 6.0 %copy-start.27 = (f32[8,50,768]{2,1,0:T(8,128)}, f32[8,50,768]{2,1,0:T(8,128)S(1)}, u32[]{:S(2)}) copy-start(f32[8,50,768]{2,1,0:T(8,128)S(1)} %get-tuple-element.105) | copy-start | bytes 3686404
  246.5 3.3 copy-start.9
  247.0 2.7 copy-start.28
  249.4 43.8 %copy-start = (f32[8,64,768]{2,1,0:T(8,128)}, f32[8,64,768]{2,1,0:T(8,128)S(1)}, u32[]{:S(2)}) copy-start(f32[8,64,768]{2,1,0:T(8,128)S(1)} %get-tuple-element.98) | copy-start | bytes 4718596
  249.7 5.9 %copy-start.42 = (f32[8,64]{1,0:T(8,128)}, f32[8,64]{1,0:T(8,128)S(1)}, u32[]{:S(2)}) copy-start(f32[8,64]{1,0:T(8,128)S(1)} %multiply_reduce_fusion.4) | copy-start | bytes 6148
  249.8 23.7 %slice-start = ((s8[14155776]{0:T(1024)(128)(4,1)}), s8[4194304]{0:T(1024)(128)(4,1)S(1)}, s32[]{:S(2)}) async-start(s8[14155776]{0:T(1024)(128)(4,1)} %bitcast.270), calls=%async_computation | async-start | bytes 8388608
  249.8 23.7 %slice-start.1 = ((s8[14155776]{0:T(1024)(128)(4,1)}), s8[4194304]{0:T(1024)(128)(4,1)S(1)}, s32[]{:S(2)}) async-start(s8[14155776]{0:T(1024)(128)(4,1)} %bitcast.270), calls=%async_computation.1 | async-start | bytes 8388608
  249.8 23.7 %slice-start.2 = ((s8[14155776]{0:T(1024)(128)(4,1)}), s8[4194304]{0:T(1024)(128)(4,1)S(1)}, s32[]{:S(2)}) async-start(s8[14155776]{0:T(1024)(128)(4,1)} %bitcast.270), calls=%async_computation.2 | async-start | bytes 8388608
  255.7 17.8 %slice-start.3 = ((s8[14155776]{0:T(1024)(128)(4,1)}), s8[1572864]{0:T(1024)(128)(4,1)S(1)}, s32[]{:S(2)}) async-start(s8[14155776]{0:T(1024)(128)(4,1)} %bitcast.270), calls=%async_computation.3 | async-start | bytes 3145728
  273.5 4.3 copy-start.25
  277.9 15.3 %copy-start.18 = (f32[8,64,3072]{2,1,0:T(8,128)}, f32[8,64,3072]{2,1,0:T(8,128)S(1)}, u32[]{:S(2)}) copy-start(f32[8,64,3072]{2,1,0:T(8,128)S(1)} %get-tuple-element.99) | copy-start | bytes 18874372
  277.9 15.3 %copy-start.55 = (f32[768]{0:T(1024)S(1)}, f32[768]{0:T(1024)}, u32[]{:S(2)}) copy-start(f32[768]{0:T(1024)} %get-tuple-element.127) | copy-start | bytes 9220
  293.1 2.7 copy-start.12
  299.0 29.0 %copy-start.59 = (f32[32]{0:T(128)S(1)}, f32[32]{0:T(128)}, u32[]{:S(2)}) copy-start(f32[32]{0:T(128)} %copy-done.58) | copy-start | bytes 388
  299.1 29.1 %copy-start.41 = (f32[8,4]{1,0:T(8,128)S(1)}, f32[8,4]{1,0:T(8,128)}, u32[]{:S(2)}) copy-start(f32[8,4]{1,0:T(8,128)} %copy-done.40) | copy-start | bytes 388
  331.1 7.2 %copy-start.26 = (bf16[8,64,768]{2,1,0:T(8,128)(2,1)S(1)}, bf16[8,64,768]{2,1,0:T(8,128)(2,1)}, u32[]{:S(2)}) copy-start(bf16[8,64,768]{2,1,0:T(8,128)(2,1)} %get-tuple-element.45) | copy-start | bytes 2359300
  336.4 110.6 %collective-permute-start.3 = (bf16[96,3072]{1,0:T(8,128)(2,1)}, bf16[96,3072]{1,0:T(8,128)(2,1)}, u32[]{:S(2)}, u32[]{:S(2)}) collective-permute-start(bf16[96,3072]{1,0:T(8,128)(2,1)} %dynamic-slice_convert_fusion), channel_id=1, source_target_pairs={{0,4},{4,0},{8,12},{12,8},{16,20},{20,16},{24,28},{28,24},{1,5},{5... | collective-permute-start | bytes 1769480 | tf_op jit(solution)/shard_map/ppermute | solution.py:558
  347.9 4.5 copy-start.1
  352.3 7.0 %copy-start.10 = (bf16[8,12,64,64]{3,2,1,0:T(8,128)(2,1)S(1)}, bf16[8,12,64,64]{3,2,1,0:T(8,128)(2,1)}, u32[]{:S(2)}) copy-start(bf16[8,12,64,64]{3,2,1,0:T(8,128)(2,1)} %copy-done.9) | copy-start | bytes 2359300
  352.3 94.7 %collective-permute-start.2 = (bf16[96,3072]{1,0:T(8,128)(2,1)}, bf16[96,3072]{1,0:T(8,128)(2,1)}, u32[]{:S(2)}, u32[]{:S(2)}) collective-permute-start(bf16[96,3072]{1,0:T(8,128)(2,1)} %dynamic-slice_convert_fusion.1), channel_id=1, source_target_pairs={{0,4},{4,0},{8,12},{12,8},{16,20},{20,16},{24,28},{28,24},{1,5},{5... | collective-permute-start | bytes 1769480 | tf_op jit(solution)/shard_map/ppermute | solution.py:558
  359.3 6.1 %copy-start.43 = (f32[8,64]{1,0:T(8,128)S(1)}, f32[8,64]{1,0:T(8,128)}, u32[]{:S(2)}) copy-start(f32[8,64]{1,0:T(8,128)} %copy-done.42) | copy-start | bytes 6148
  365.3 3.4 copy-start.2
  365.3 3.4 copy-start.19
  375.2 65.6 %collective-permute-start.1 = (bf16[96,768]{1,0:T(8,128)(2,1)}, bf16[96,768]{1,0:T(8,128)(2,1)S(1)}, u32[]{:S(2)}, u32[]{:S(2)}) collective-permute-start(bf16[96,768]{1,0:T(8,128)(2,1)} %dynamic-slice_convert_fusion.3), channel_id=1, source_target_pairs={{0,4},{4,0},{8,12},{12,8},{16,20},{20,16},{24,28},{28,24},{1,5},{5... | collective-permute-start | bytes 442376 | tf_op jit(solution)/shard_map/ppermute | solution.py:558
  400.9 7.7 %copy-start.5 = (f32[4,128,768]{2,1,0:T(8,128)S(1)}, f32[4,128,768]{2,1,0:T(8,128)}, u32[]{:S(2)}) copy-start(f32[4,128,768]{2,1,0:T(8,128)} %copy-done.3) | copy-start | bytes 4718596
  400.9 7.7 %copy-start.52 = (f32[512]{0:T(512)S(1)}, f32[512]{0:T(512)}, u32[]{:S(2)}) copy-start(f32[512]{0:T(512)} %get-tuple-element.87) | copy-start | bytes 6148
  400.9 7.7 %copy-start.53 = (f32[512]{0:T(512)S(1)}, f32[512]{0:T(512)}, u32[]{:S(2)}) copy-start(f32[512]{0:T(512)} %get-tuple-element.89) | copy-start | bytes 6148
  412.9 30.6 %collective-permute-start = (bf16[96,2304]{1,0:T(8,128)(2,1)S(1)}, bf16[96,2304]{1,0:T(8,128)(2,1)}, u32[]{:S(2)}, u32[]{:S(2)}) collective-permute-start(bf16[96,2304]{1,0:T(8,128)(2,1)S(1)} %dynamic-slice_convert_fusion.2), channel_id=1, source_target_pairs={{0,4},{4,0},{8,12},{12,8},{16,20},{20,16},{24,28},{28,24},{1,5},{5... | collective-permute-start | bytes 1327112 | tf_op jit(solution)/shard_map/ppermute | solution.py:558
  429.9 7.0 %copy-start.15 = (bf16[8,64,2304]{2,1,0:T(8,128)(2,1)S(1)}, bf16[8,64,2304]{2,1,0:T(8,128)(2,1)}, u32[]{:S(2)}) copy-start(bf16[8,64,2304]{2,1,0:T(8,128)(2,1)} %convert_element_type.227) | copy-start | bytes 7077892
  434.2 7.3 %copy-start.24 = (f32[192,768]{1,0:T(8,128)S(1)}, f32[192,768]{1,0:T(8,128)}, u32[]{:S(2)}) copy-start(f32[192,768]{1,0:T(8,128)} %copy-done.23) | copy-start | bytes 1769476
  447.0 3.2 copy-start.29
  479.8 9.6 %copy-start.45 = (f32[768]{0:T(1024)S(1)}, f32[768]{0:T(1024)}, u32[]{:S(2)}) copy-start(f32[768]{0:T(1024)} %get-tuple-element.44) | copy-start | bytes 9220
  484.1 5.1 copy-start.48
  484.1 5.2 copy-start.57
  484.1 5.2 copy-start.50
  484.1 5.2 copy-start.49
  484.2 5.2 copy-start.47
  484.2 5.2 copy-start.46
  484.2 5.3 copy-start.56
  484.2 5.3 copy-start.51
  517.3 7.5 %copy-start.30 = (f32[9216]{0:T(1024)S(1)}, f32[9216]{0:T(1024)}, u32[]{:S(2)}) copy-start(f32[9216]{0:T(1024)} %param.17) | copy-start | bytes 110596
  517.3 7.5 %copy-start.32 = (f32[3,24,128]{2,1,0:T(8,128)S(1)}, f32[3,24,128]{2,1,0:T(8,128)}, u32[]{:S(2)}) copy-start(f32[3,24,128]{2,1,0:T(8,128)} %slice.307) | copy-start | bytes 110596
  517.3 7.6 %copy-start.44 = (f32[9216]{0:T(1024)S(1)}, f32[9216]{0:T(1024)}, u32[]{:S(2)}) copy-start(f32[9216]{0:T(1024)} %param.19) | copy-start | bytes 110596
  517.3 8.2 %copy-start.11 = (f32[96,9216]{1,0:T(8,128)S(1)}, f32[96,9216]{1,0:T(8,128)}, u32[]{:S(2)}) copy-start(f32[96,9216]{1,0:T(8,128)} %param.16) | copy-start | bytes 10616836
  (20 other events, 24.6 us)
